TPU v7x, 32 devices: a whole 2x2x4 slice. The times are simulated.
32 devices in a mesh: wave: 8 (over z, y), lev: 4 (over x, core).
Axes of the slice: x: 2, y: 2, z: 4, core: 2. Of those that a mesh axis runs over, the one named last changes fastest.
Arguments:
- fine_state: float32 [8, 3, 2, 24, 49], P('lev', None, None, 'wave'), may hold values from -6 to 6
- fold_pairs: int32 [24], replicated, may hold values from 0 to 23, each once
- legendre: bfloat16 [24, 96, 49], P('wave', 'lev'), may hold values from -0.875 to 0.875
- gauss_weights: float32 [96], P('lev'), may hold values from 0.5 to 3
- grid_coef: float32 [8, 2560], replicated, may hold values from -4 to 4
- modes_from: float32 [8, 8], replicated
- modes_to: float32 [8, 8], replicated, as said below
- mode_rates: float32 [8], replicated, may hold values from 0.2 to 20
Outputs:
- corrected: float32 [8, 2, 2, 24, 49], P('lev', None, None, 'wave')
- fine_tend: float32 [8, 3, 2, 24, 49], P('lev', None, None, 'wave')
Inputs may be any that keep to these rules, and one draw needn't show every extreme that they name: Slot p holds zonal wavenumbers fold_pairs[p] and 47 - fold_pairs[p]; every value occurs once. modes_to is the inverse of modes_from.
All inputs are finite; a program needn't handle non-finite values.
Results may differ from a plain program's by a relative error of at most 0.02.
Values may be sent and summed in bfloat16 or wider, within the bound.
No kernel may reach another device: no remote copies, remote signals or barrier semaphores. Data moves between devices by JAX's collectives and lax.ppermute only.
A program may use at most 64 MiB of HBM per device.

v0:
```python
import math
import jax
import jax.numpy as jnp
from jax import lax
from jax.sharding import PartitionSpec as P

STEP_HALF = 0.5
quad_weights = ((5.0 / 24.0, 1.0 / 3.0, -1.0 / 24.0), (-1.0 / 24.0, 1.0 / 3.0, 5.0 / 24.0))
HIGHEST = lax.Precision.HIGHEST


def fourier_table(waves, points, amplitude):
    steps = jnp.arange(points, dtype=jnp.int32)
    turns = waves[:, :, None] * steps[None, None, :] % points
    angles = turns.astype(jnp.float32) * (2.0 * math.pi / points)
    return jnp.stack([jnp.cos(angles) * amplitude, -jnp.sin(angles) * amplitude]).astype(
        jnp.bfloat16
    )


def fine_rows(small_wave, fine_width):
    row_ids = jnp.arange(fine_width + 1, dtype=jnp.int32)[None, :]
    return row_ids < fine_width - small_wave[:, None]


def coarse_rows(small_wave, coarse):
    row_ids = jnp.arange(coarse, dtype=jnp.int32)[None, :]
    coarse_keep = row_ids < coarse - small_wave[:, None]
    degree = (small_wave[:, None] + row_ids).astype(jnp.float32)
    return (coarse_keep, degree)


def legendre_inverse(spectral, legendre_table, row_mask):
    split_spec = spectral[:, :, :, :, None, :] * row_mask[None, None, None]
    return jnp.einsum(
        "abcpmr,plr->abcpml", split_spec, legendre_table, preferred_element_type=jnp.float32
    ).astype(jnp.bfloat16)


def legendre_forward(returned, legendre_table, row_mask):
    members = jnp.einsum(
        "abcpml,plr->abcpmr", returned, legendre_table, preferred_element_type=jnp.float32
    )
    return jnp.sum(members * row_mask.astype(jnp.float32)[None, None, None], axis=4)


def grid_step(fourier, wave_table, coef, weights, factor):
    grid_field = jnp.einsum(
        "abcpmz,cpmk->abzk", fourier, wave_table, preferred_element_type=jnp.float32
    )
    product = (coef[:, None, None, :] * grid_field * grid_field).astype(jnp.bfloat16)
    returned = jnp.einsum(
        "abzk,cpmk->abcpmz", product, wave_table, preferred_element_type=jnp.float32
    )
    return (returned * (weights * factor)).astype(jnp.bfloat16)


def mix(matrix, values):
    return jnp.einsum("ql,lbcpr->qbcpr", matrix, values, precision=HIGHEST)


def per_device(
    fine_state, fold_pairs, legendre, gauss_weights, grid_coef, modes_from, modes_to, mode_rates
):
    n_wave = lax.axis_size("wave")
    wave_idx = lax.axis_index("wave")
    lev_idx = lax.axis_index("lev")
    lev_dev = fine_state.shape[0]
    pairs_dev = fine_state.shape[3]
    fine_width = fine_state.shape[4] - 1
    coarse = fine_width // 2
    longitudes = grid_coef.shape[1]
    band_size = legendre.shape[1] // n_wave
    small_wave = lax.dynamic_slice_in_dim(fold_pairs, wave_idx * pairs_dev, pairs_dev)
    first_member = fine_rows(small_wave, fine_width)
    member_mask = jnp.stack([first_member, jnp.logical_not(first_member)], 1).astype(jnp.bfloat16)
    coarse_keep, degree = coarse_rows(small_wave, coarse)
    keep_mask = coarse_keep[:, None, :].astype(jnp.bfloat16)
    keep_float = coarse_keep.astype(jnp.float32)
    fine_table = fourier_table(
        jnp.stack([fold_pairs, fine_width - 1 - fold_pairs], 1), longitudes, fine_width ** (-0.5)
    )
    coarse_table = fourier_table(fold_pairs[:, None], longitudes // 2, coarse ** (-0.5))
    coarse_leg = legendre[:, :, :coarse]
    coarse_coef = grid_coef[:, ::2]
    band_gauss = lax.dynamic_slice_in_dim(gauss_weights, wave_idx * band_size, band_size)
    local_to = lax.dynamic_slice_in_dim(modes_to, lev_idx * lev_dev, lev_dev, 1)
    local_from = lax.dynamic_slice_in_dim(modes_from, lev_idx * lev_dev, lev_dev, 1)
    mode_decay = lax.dynamic_slice_in_dim(mode_rates, lev_idx * lev_dev, lev_dev)

    def project(partial_sum):
        return mix(modes_to, partial_sum)

    def coarse_start(modes):
        gathered = lax.all_gather(modes, "lev", axis=0, tiled=True)
        levels = (mix(modes_from, gathered) * keep_float).astype(jnp.bfloat16)
        return legendre_inverse(levels, coarse_leg, keep_mask)

    def coarse_grid_step(fourier):
        return grid_step(
            fourier, coarse_table, coarse_coef, band_gauss, 2.0 * coarse / (longitudes // 2)
        )

    def coarse_finish(returned):
        partial_sum = legendre_forward(returned, coarse_leg, keep_mask)
        return lax.psum_scatter(
            project(partial_sum).astype(jnp.bfloat16), "lev", scatter_dimension=0, tiled=True
        ).astype(jnp.float32)

    def coarse_eval(modes):
        fourier = lax.all_to_all(
            coarse_start(modes), "wave", split_axis=5, concat_axis=3, tiled=True
        )
        returned = lax.all_to_all(
            coarse_grid_step(fourier), "wave", split_axis=3, concat_axis=5, tiled=True
        )
        return coarse_finish(returned)

    restricted = fine_state[..., :coarse] * keep_float
    fine_spec = lax.all_gather(fine_state.astype(jnp.bfloat16), "lev", axis=0, tiled=True)
    fine_fourier = legendre_inverse(fine_spec, legendre, member_mask)
    fine_fourier = lax.all_to_all(fine_fourier, "wave", split_axis=5, concat_axis=3, tiled=True)
    fine_back = lax.all_to_all(
        grid_step(fine_fourier, fine_table, grid_coef, band_gauss, 2.0 * fine_width / longitudes),
        "wave",
        split_axis=3,
        concat_axis=5,
        tiled=True,
    )
    fine_tend = lax.psum_scatter(
        legendre_forward(fine_back, legendre, member_mask).astype(jnp.bfloat16),
        "lev",
        scatter_dimension=0,
        tiled=True,
    ).astype(jnp.float32)
    restricted_tend = fine_tend[..., :coarse] * keep_float
    stacked = jnp.concatenate([restricted, restricted_tend], 1)
    both_modes = lax.psum_scatter(
        mix(local_to, stacked).astype(jnp.bfloat16), "lev", scatter_dimension=0, tiled=True
    ).astype(jnp.float32)
    nodes = fine_state.shape[1]
    old_state = both_modes[:, :nodes]
    old_tend = both_modes[:, nodes:]
    old_coarse = coarse_eval(old_state[:, 1:2])
    stiffness = (
        mode_decay[:, None, None, None]
        * (degree * (degree + 1.0) / (coarse * (coarse + 1.0)))[None, None]
    )
    source = old_tend - stiffness[:, None] * old_state
    integral_mid = (
        quad_weights[0][0] * source[:, 0]
        + quad_weights[0][1] * source[:, 1]
        + quad_weights[0][2] * source[:, 2]
    )
    integral_end = (
        quad_weights[1][0] * source[:, 0]
        + quad_weights[1][1] * source[:, 1]
        + quad_weights[1][2] * source[:, 2]
    )
    divisor = 1.0 + STEP_HALF * stiffness
    next_mid = (old_state[:, 0] + STEP_HALF * stiffness * old_state[:, 1] + integral_mid) / divisor
    coarse_fresh = coarse_eval(next_mid[:, None])
    next_end = (
        next_mid
        + STEP_HALF * (coarse_fresh[:, 0] - old_coarse[:, 0])
        + STEP_HALF * stiffness * old_state[:, 2]
        + integral_end
    ) / divisor
    change = jnp.stack([next_mid - old_state[:, 1], next_end - old_state[:, 2]], 1)
    lifted = lax.psum_scatter(
        mix(local_from, change).astype(jnp.bfloat16), "lev", scatter_dimension=0, tiled=True
    ).astype(jnp.float32)
    corrected = fine_state[:, 1:] + jnp.pad(
        lifted, ((0, 0), (0, 0), (0, 0), (0, 0), (0, fine_width + 1 - coarse))
    )
    return (corrected, fine_tend)


def solution(mesh):
    placed = (
        P("lev", None, None, "wave", None),
        P(),
        P("wave", "lev", None),
        P("lev"),
        P(),
        P(),
        P(),
        P(),
    )
    return jax.shard_map(
        per_device,
        mesh=mesh,
        in_specs=placed,
        out_specs=(P("lev", None, None, "wave", None), P("lev", None, None, "wave", None)),
        check_vma=False,
    )
```

profile of v0, /device:TPU:0, one launch (start us, length us, event | category | flops | bytes accessed | tf_op | source)
XLA Modules:
  0.0 130.4 jit_solution(1549815140402897033)
XLA Ops:
  1.5 6.2 %all_gather.9 = bf16[8,3,2,3,49]{4,2,3,1,0:T(2,128)(2,1)S(1)} all-gather(bf16[2,3,2,3,49]{4,2,3,1,0:T(2,128)(2,1)S(1)} %convert_element_type.212), channel_id=1, replica_groups=mesh['wave'=8,'lev'=4] {'lev'}, dimensions={0}, use_global_device_ids=true | all-gather | bytes 17640 | tf_op jit(solution)/shard_map/all_gather | solution.py:120
  8.7 0.8 reshape.468
  9.6 6.4 %all-to-all-start = ((bf16[8,2,432]{2,1,0:T(2,128)(2,1)}), bf16[8,2,432]{2,1,0:T(2,128)(2,1)S(1)}, u32[]{:S(2)}, u32[]{:S(2)}) async-start(bf16[8,2,432]{2,1,0:T(2,128)(2,1)} %reshape.468), calls=%async_computation | async-start | bytes 32768 | tf_op jit(solution)/shard_map/all_to_all | solution.py:122
  16.7 2.3 %multiply_convert_fusion.1 = (bf16[1,24,2,2560]{3,1,2,0:T(8,128)(2,1)S(1)}, bf16[1,24,2,2560]{3,1,2,0:T(8,128)(2,1)S(1)}) fusion(s32[24,2]{0,1:T(2,128)S(1)} %pad_add_fusion), kind=kLoop, calls=%fused_computation.52 | loop fusion | flops 1720320 | bytes 491712 | tf_op jit(solution)/shard_map/convert.4
  20.5 2.1 %all-to-all-done = bf16[8,2,432]{2,1,0:T(2,128)(2,1)S(1)} async-done(((bf16[8,2,432]{2,1,0:T(2,128)(2,1)}), bf16[8,2,432]{2,1,0:T(2,128)(2,1)S(1)}, u32[]{:S(2)}, u32[]{:S(2)}) %all-to-all-start) | async-done | bytes 13856 | tf_op jit(solution)/shard_map/all_to_all | solution.py:122
  23.7 0.8 fusion.3
  24.7 0.8 reshape.470
  25.6 3.9 %all-to-all-start.1 = ((bf16[8,2,432]{2,1,0:T(2,128)(2,1)}), bf16[8,2,432]{2,1,0:T(2,128)(2,1)S(1)}, u32[]{:S(2)}, u32[]{:S(2)}) async-start(bf16[8,2,432]{2,1,0:T(2,128)(2,1)} %reshape.470), calls=%async_computation.1 | async-start | bytes 32768 | tf_op jit(solution)/shard_map/all_to_all | solution.py:123
  29.5 1.4 %slice.58 = f32[8,1280]{1,0:T(8,128)S(1)} slice(f32[8,2560]{1,0:T(8,128)S(1)} %copy-done.3), slice={[0:8:1], [0:2560:2]} | slice | bytes 81920 | tf_op jit(solution)/shard_map/slice | solution.py:85
  32.9 3.2 %all-to-all-done.1 = bf16[8,2,432]{2,1,0:T(2,128)(2,1)S(1)} async-done(((bf16[8,2,432]{2,1,0:T(2,128)(2,1)}), bf16[8,2,432]{2,1,0:T(2,128)(2,1)S(1)}, u32[]{:S(2)}, u32[]{:S(2)}) %all-to-all-start.1) | async-done | bytes 13856 | tf_op jit(solution)/shard_map/all_to_all | solution.py:123
  36.7 10.5 %all-reduce.1 = bf16[8,3,2,3,49]{4,0,3,2,1:T(8,128)(2,1)S(1)} all-reduce(bf16[8,3,2,3,49]{4,0,3,2,1:T(8,128)(2,1)S(1)} %copy.103), channel_id=2, replica_groups=mesh['wave'=8,'lev'=4] {'lev'}, use_global_device_ids=true, to_apply=%region_1.2.clone | all-reduce | flops 7056 | bytes 28224
  47.6 11.7 %all-reduce.2 = bf16[8,6,2,3,24]{4,0,3,2,1:T(8,128)(2,1)S(1)} all-reduce(bf16[8,6,2,3,24]{4,0,3,2,1:T(8,128)(2,1)S(1)} %convolution_convert_fusion), channel_id=3, replica_groups=mesh['wave'=8,'lev'=4] {'lev'}, use_global_device_ids=true, to_apply=%region_2.3.clone | all-reduce | flops 6912 | bytes 27648
  59.4 5.2 %all_gather.10 = f32[8,1,2,3,24]{4,2,3,1,0:T(2,128)S(1)} all-gather(f32[2,1,2,3,24]{4,2,3,1,0:T(2,128)S(1)} %copy.104), channel_id=1, replica_groups=mesh['wave'=8,'lev'=4] {'lev'}, dimensions={0}, use_global_device_ids=true | all-gather | bytes 5760 | tf_op jit(solution)/shard_map/all_gather | solution.py:95
  65.6 3.3 %all-to-all-start.2 = ((bf16[8,1,2,3,1,24]{0,2,3,4,1,5:T(2,128)(2,1)}), bf16[8,1,2,3,1,24]{0,2,3,4,1,5:T(2,128)(2,1)S(1)}, u32[]{:S(2)}, u32[]{:S(2)}) async-start(bf16[8,1,2,3,1,24]{0,2,3,4,1,5:T(2,128)(2,1)} %copy.106), calls=%async_computation.2 | async-start | bytes 73728 | tf_op jit(solution)/shard_map/all_to_all | solution.py:111
  69.0 5.2 %all_gather.11 = f32[8,1,2,3,24]{4,2,3,1,0:T(2,128)S(1)} all-gather(f32[2,1,2,3,24]{4,2,3,1,0:T(2,128)S(1)} %copy.114), channel_id=1, replica_groups=mesh['wave'=8,'lev'=4] {'lev'}, dimensions={0}, use_global_device_ids=true | all-gather | bytes 5760 | tf_op jit(solution)/shard_map/all_gather | solution.py:95
  75.8 5.9 %all-to-all-start.4 = ((bf16[8,1,2,3,1,24]{0,2,3,4,1,5:T(2,128)(2,1)}), bf16[8,1,2,3,1,24]{0,2,3,4,1,5:T(2,128)(2,1)S(1)}, u32[]{:S(2)}, u32[]{:S(2)}) async-start(bf16[8,1,2,3,1,24]{0,2,3,4,1,5:T(2,128)(2,1)} %copy.116), calls=%async_computation.4 | async-start | bytes 73728 | tf_op jit(solution)/shard_map/all_to_all | solution.py:111
  82.2 0.8 copy.110
  82.9 5.5 %all-to-all-done.4 = bf16[8,1,2,3,1,24]{0,2,3,4,1,5:T(2,128)(2,1)S(1)} async-done(((bf16[8,1,2,3,1,24]{0,2,3,4,1,5:T(2,128)(2,1)}), bf16[8,1,2,3,1,24]{0,2,3,4,1,5:T(2,128)(2,1)S(1)}, u32[]{:S(2)}, u32[]{:S(2)}) %all-to-all-start.4) | async-done | bytes 2336 | tf_op jit(solution)/shard_map/all_to_all | solution.py:111
  88.4 3.3 %all-to-all-start.3 = ((bf16[8,1,2,24,1,3]{0,2,5,4,1,3:T(2,128)(2,1)}), bf16[8,1,2,24,1,3]{0,2,5,4,1,3:T(2,128)(2,1)S(1)}, u32[]{:S(2)}, u32[]{:S(2)}) async-start(bf16[8,1,2,24,1,3]{0,2,5,4,1,3:T(2,128)(2,1)} %copy.110), calls=%async_computation.3 | async-start | bytes 73728 | tf_op jit(solution)/shard_map/all_to_all | solution.py:114
  93.0 5.5 %all-to-all-done.3 = bf16[8,1,2,24,1,3]{0,2,5,4,1,3:T(2,128)(2,1)S(1)} async-done(((bf16[8,1,2,24,1,3]{0,2,5,4,1,3:T(2,128)(2,1)}), bf16[8,1,2,24,1,3]{0,2,5,4,1,3:T(2,128)(2,1)S(1)}, u32[]{:S(2)}, u32[]{:S(2)}) %all-to-all-start.3) | async-done | bytes 2336 | tf_op jit(solution)/shard_map/all_to_all | solution.py:114
  98.4 3.3 %all-to-all-start.5 = ((bf16[8,1,2,24,1,3]{0,2,5,4,1,3:T(2,128)(2,1)}), bf16[8,1,2,24,1,3]{0,2,5,4,1,3:T(2,128)(2,1)S(1)}, u32[]{:S(2)}, u32[]{:S(2)}) async-start(bf16[8,1,2,24,1,3]{0,2,5,4,1,3:T(2,128)(2,1)} %copy.120), calls=%async_computation.5 | async-start | bytes 73728 | tf_op jit(solution)/shard_map/all_to_all | solution.py:114
  102.2 6.2 %all-to-all-done.5 = bf16[8,1,2,24,1,3]{0,2,5,4,1,3:T(2,128)(2,1)S(1)} async-done(((bf16[8,1,2,24,1,3]{0,2,5,4,1,3:T(2,128)(2,1)}), bf16[8,1,2,24,1,3]{0,2,5,4,1,3:T(2,128)(2,1)S(1)}, u32[]{:S(2)}, u32[]{:S(2)}) %all-to-all-start.5) | async-done | bytes 2336 | tf_op jit(solution)/shard_map/all_to_all | solution.py:114
  108.8 10.3 %all-reduce.6 = (bf16[8,1,2,3,24]{4,0,3,2,1:T(8,128)(2,1)S(1)}, bf16[8,1,2,3,24]{4,0,3,2,1:T(8,128)(2,1)S(1)}) all-reduce(bf16[8,1,2,3,24]{4,0,3,2,1:T(8,128)(2,1)S(1)} %fusion.17, bf16[8,1,2,3,24]{4,0,3,2,1:T(8,128)(2,1)S(1)} %fusion.15), channel_id=5, replica_groups=mesh['wave'=8,'lev'=4] {'lev'}, use_global_device_ids=true, to_apply=%region_4.5.clone | all-reduce | flops 2304 | bytes 9216
  119.4 10.4 %all-reduce.5 = bf16[8,2,2,3,24]{4,0,3,2,1:T(8,128)(2,1)S(1)} all-reduce(bf16[8,2,2,3,24]{4,0,3,2,1:T(8,128)(2,1)S(1)} %convolution_convert_fusion.2), channel_id=6, replica_groups=mesh['wave'=8,'lev'=4] {'lev'}, use_global_device_ids=true, to_apply=%region_5.6.clone | all-reduce | flops 2304 | bytes 9216
  (77 shorter events, 13.5 us)
Async XLA Ops:
  0.6 46.6 %copy-start = (f32[8,8]{1,0:T(8,128)S(1)}, f32[8,8]{1,0:T(8,128)}, u32[]{:S(2)}) copy-start(f32[8,8]{1,0:T(8,128)} %param.14) | copy-start | bytes 772
  0.6 0.8 copy-start.2
  7.7 0.7 copy-start.1
  9.6 6.4 %copy-start.5 = (s32[24]{0:T(128)S(1)}, s32[24]{0:T(128)}, u32[]{:S(2)}) copy-start(s32[24]{0:T(128)} %param.9) | copy-start | bytes 292
  9.6 13.0 %all-to-all-start = ((bf16[8,2,432]{2,1,0:T(2,128)(2,1)}), bf16[8,2,432]{2,1,0:T(2,128)(2,1)S(1)}, u32[]{:S(2)}, u32[]{:S(2)}) async-start(bf16[8,2,432]{2,1,0:T(2,128)(2,1)} %reshape.468), calls=%async_computation | async-start | bytes 32768 | tf_op jit(solution)/shard_map/all_to_all | solution.py:122
  19.0 0.7 copy-start.6
  19.8 0.7 copy-start.7
  22.8 0.9 copy-start.3
  25.6 10.5 %all-to-all-start.1 = ((bf16[8,2,432]{2,1,0:T(2,128)(2,1)}), bf16[8,2,432]{2,1,0:T(2,128)(2,1)S(1)}, u32[]{:S(2)}, u32[]{:S(2)}) async-start(bf16[8,2,432]{2,1,0:T(2,128)(2,1)} %reshape.470), calls=%async_computation.1 | async-start | bytes 32768 | tf_op jit(solution)/shard_map/all_to_all | solution.py:123
  31.0 0.7 copy-start.8
  59.3 5.3 %copy-start.4 = (f32[8,8]{1,0:T(8,128)S(1)}, f32[8,8]{1,0:T(8,128)}, u32[]{:S(2)}) copy-start(f32[8,8]{1,0:T(8,128)} %param.13) | copy-start | bytes 772
  65.6 10.2 %all-to-all-start.2 = ((bf16[8,1,2,3,1,24]{0,2,3,4,1,5:T(2,128)(2,1)}), bf16[8,1,2,3,1,24]{0,2,3,4,1,5:T(2,128)(2,1)S(1)}, u32[]{:S(2)}, u32[]{:S(2)}) async-start(bf16[8,1,2,3,1,24]{0,2,3,4,1,5:T(2,128)(2,1)} %copy.106), calls=%async_computation.2 | async-start | bytes 73728 | tf_op jit(solution)/shard_map/all_to_all | solution.py:111
  75.8 12.6 %all-to-all-start.4 = ((bf16[8,1,2,3,1,24]{0,2,3,4,1,5:T(2,128)(2,1)}), bf16[8,1,2,3,1,24]{0,2,3,4,1,5:T(2,128)(2,1)S(1)}, u32[]{:S(2)}, u32[]{:S(2)}) async-start(bf16[8,1,2,3,1,24]{0,2,3,4,1,5:T(2,128)(2,1)} %copy.116), calls=%async_computation.4 | async-start | bytes 73728 | tf_op jit(solution)/shard_map/all_to_all | solution.py:111
  88.4 10.0 %all-to-all-start.3 = ((bf16[8,1,2,24,1,3]{0,2,5,4,1,3:T(2,128)(2,1)}), bf16[8,1,2,24,1,3]{0,2,5,4,1,3:T(2,128)(2,1)S(1)}, u32[]{:S(2)}, u32[]{:S(2)}) async-start(bf16[8,1,2,24,1,3]{0,2,5,4,1,3:T(2,128)(2,1)} %copy.110), calls=%async_computation.3 | async-start | bytes 73728 | tf_op jit(solution)/shard_map/all_to_all | solution.py:114
  98.4 10.0 %all-to-all-start.5 = ((bf16[8,1,2,24,1,3]{0,2,5,4,1,3:T(2,128)(2,1)}), bf16[8,1,2,24,1,3]{0,2,5,4,1,3:T(2,128)(2,1)S(1)}, u32[]{:S(2)}, u32[]{:S(2)}) async-start(bf16[8,1,2,24,1,3]{0,2,5,4,1,3:T(2,128)(2,1)} %copy.120), calls=%async_computation.5 | async-start | bytes 73728 | tf_op jit(solution)/shard_map/all_to_all | solution.py:114
where the time goes:
time: 131 us; the launch traced here: 130 us
  blocking collectives  59.5 us (45%)
  starting transfers between devices  26.3 us (20%)
  waiting for transfers between devices  22.5 us (17%)
  local copies, waits for them, and re-layouts  12.5 us (10%)
  other arithmetic  4.17 us (3%)
  matrix products  3.8 us (3%)
  between operations  1.69 us (1%)
    unnamed x4, blocking collectives  42.8 us
    all_to_all x2, waiting for transfers between devices, coarse_eval(): lax.all_to_all(coarse_grid_step(fourier), 'wave', split_axis=3, concat_ax...  11.7 us
    all_gather x2, blocking collectives, coarse_start(): gathered = lax.all_gather(modes, 'lev', axis=0, tiled=True)  10.4 us
    all_to_all x2, starting transfers between devices, coarse_eval(): lax.all_to_all(coarse_start(modes), 'wave', split_axis=5, concat_axis=3,...  9.25 us
    unnamed x26, local copies, waits for them, and re-layouts  7.27 us
    all_to_all x2, starting transfers between devices, coarse_eval(): lax.all_to_all(coarse_grid_step(fourier), 'wave', split_axis=3, concat_ax...  6.68 us
    all_to_all x1, starting transfers between devices, per_device(): lax.all_to_all(fine_fourier, 'wave', split_axis=5, concat_axis=3, tiled=T...  6.43 us
    all_gather x1, blocking collectives, per_device(): lax.all_gather(fine_state.astype(jnp.bfloat16), 'lev', axis=0, tiled=True)  6.21 us
  transfers between devices with their start and end apart: 6, of which 5 were waited for; matrix products, arithmetic and copies ran while one was open for 7% of the time, Pallas kernels for 0%

commit v1 on v0

--- a/solution.py
+++ b/solution.py
@@ -3,10 +3,25 @@
 import jax.numpy as jnp
 from jax import lax
 from jax.sharding import PartitionSpec as P
+from jax.lax import axis_index, ppermute, psum
 
 STEP_HALF = 0.5
 quad_weights = ((5.0 / 24.0, 1.0 / 3.0, -1.0 / 24.0), (-1.0 / 24.0, 1.0 / 3.0, 5.0 / 24.0))
 HIGHEST = lax.Precision.HIGHEST
+
+
+def _draw_vector(q_in, net_axis):
+    many = psum(1, net_axis)
+    by_place = []
+    for u in [*range(many)]:
+        by_place.append((u, (u + 1) % many))
+    arr_now = [None] * many
+    arr_now[many - 1] = q_in
+    for dev_i in range(many - 2, -1, -1):
+        arr_now[dev_i] = ppermute(arr_now[dev_i + 1], net_axis, by_place)
+    block_last = jnp.concatenate(arr_now, 0)
+    piece_now = axis_index(net_axis)
+    return jnp.roll(block_last, (piece_now + 1) * q_in.shape[0], 0)
 
 
 def fourier_table(waves, points, amplitude):
@@ -92,7 +107,7 @@
         return mix(modes_to, partial_sum)
 
     def coarse_start(modes):
-        gathered = lax.all_gather(modes, "lev", axis=0, tiled=True)
+        gathered = _draw_vector(modes, net_axis="lev")
         levels = (mix(modes_from, gathered) * keep_float).astype(jnp.bfloat16)
         return legendre_inverse(levels, coarse_leg, keep_mask)
 

time: 131 us -> 132 us (level)
  waiting for transfers between devices: 22.5 us -> 33.2 us
  blocking collectives: 59.5 us -> 49.1 us
    all_gather x2 -> x0, blocking collectives: 10.4 us -> none  [coarse_start(): gathered = lax.all_gather(modes, 'lev', axis=0, tiled=True)]
    all_to_all x2, waiting for transfers between devices: 5.53 us -> 11 us  [coarse_eval(): lax.all_to_all(coarse_start(modes), 'wave', split_axis=5, concat_axis=3,...]
    ppermute x0 -> x6, starting transfers between devices: none -> 3.48 us  [_draw_vector(): arr_now[dev_i] = ppermute(arr_now[dev_i + 1], net_axis, by_place)]
    ppermute x0 -> x6, waiting for transfers between devices: none -> 3.22 us  [_draw_vector(): arr_now[dev_i] = ppermute(arr_now[dev_i + 1], net_axis, by_place)]
    all_to_all x2, starting transfers between devices: 9.25 us -> 6.68 us  [coarse_eval(): lax.all_to_all(coarse_start(modes), 'wave', split_axis=5, concat_axis=3,...]
    all_to_all x1, waiting for transfers between devices: 3.18 us -> 4.57 us  [per_device(): lax.all_to_all(grid_step(fine_fourier, fine_table, grid_coef, band_gauss,...]
  transfers between devices with their start and end apart: 6 -> 12, of which waited for: 5 -> 8; matrix products, arithmetic and copies ran while one was open for 7% -> 8% of each run, Pallas kernels for 0% -> 0%
where the time goes in v1:
time: 132 us; the launch traced here: 131 us
  blocking collectives  49.1 us (37%)
  waiting for transfers between devices  33.2 us (25%)
  starting transfers between devices  26.6 us (20%)
  local copies, waits for them, and re-layouts  12.5 us (9%)
  other arithmetic  4.17 us (3%)
  matrix products  3.97 us (3%)
  between operations  1.71 us (1%)
    unnamed x4, blocking collectives  42.8 us
    all_to_all x2, waiting for transfers between devices, coarse_eval(): lax.all_to_all(coarse_grid_step(fourier), 'wave', split_axis=3, concat_ax...  11.7 us
    all_to_all x2, waiting for transfers between devices, coarse_eval(): lax.all_to_all(coarse_start(modes), 'wave', split_axis=5, concat_axis=3,...  11 us
    unnamed x26, local copies, waits for them, and re-layouts  7.27 us
    all_to_all x2, starting transfers between devices, coarse_eval(): lax.all_to_all(coarse_grid_step(fourier), 'wave', split_axis=3, concat_ax...  6.68 us
    all_to_all x2, starting transfers between devices, coarse_eval(): lax.all_to_all(coarse_start(modes), 'wave', split_axis=5, concat_axis=3,...  6.68 us
    all_to_all x1, starting transfers between devices, per_device(): lax.all_to_all(fine_fourier, 'wave', split_axis=5, concat_axis=3, tiled=T...  6.43 us
    all_gather x1, blocking collectives, per_device(): lax.all_gather(fine_state.astype(jnp.bfloat16), 'lev', axis=0, tiled=True)  6.21 us
  transfers between devices with their start and end apart: 12, of which 8 were waited for; matrix products, arithmetic and copies ran while one was open for 8% of the time, Pallas kernels for 0%

profile of v1, /device:TPU:0, one launch (start us, length us, event | category | flops | bytes accessed | tf_op | source)
XLA Modules:
  0.0 131.2 jit_solution(15487430890582110499)
XLA Ops:
  1.5 6.2 %all_gather.3 = bf16[8,3,2,3,49]{4,2,3,1,0:T(2,128)(2,1)S(1)} all-gather(bf16[2,3,2,3,49]{4,2,3,1,0:T(2,128)(2,1)S(1)} %convert_element_type.212), channel_id=1, replica_groups=mesh['wave'=8,'lev'=4] {'lev'}, dimensions={0}, use_global_device_ids=true | all-gather | bytes 17640 | tf_op jit(solution)/shard_map/all_gather | solution.py:135
  9.6 6.4 %all-to-all-start = ((bf16[8,2,432]{2,1,0:T(2,128)(2,1)}), bf16[8,2,432]{2,1,0:T(2,128)(2,1)S(1)}, u32[]{:S(2)}, u32[]{:S(2)}) async-start(bf16[8,2,432]{2,1,0:T(2,128)(2,1)} %reshape.468), calls=%async_computation | async-start | bytes 32768 | tf_op jit(solution)/shard_map/all_to_all | solution.py:137
  16.1 2.3 %multiply_convert_fusion.1 = (bf16[1,24,2,2560]{3,1,2,0:T(8,128)(2,1)S(1)}, bf16[1,24,2,2560]{3,1,2,0:T(8,128)(2,1)S(1)}) fusion(s32[24,2]{0,1:T(2,128)S(1)} %pad_add_fusion), kind=kLoop, calls=%fused_computation.52 | loop fusion | flops 1720320 | bytes 491712 | tf_op jit(solution)/shard_map/convert.4
  19.9 2.7 %all-to-all-done = bf16[8,2,432]{2,1,0:T(2,128)(2,1)S(1)} async-done(((bf16[8,2,432]{2,1,0:T(2,128)(2,1)}), bf16[8,2,432]{2,1,0:T(2,128)(2,1)S(1)}, u32[]{:S(2)}, u32[]{:S(2)}) %all-to-all-start) | async-done | bytes 13856 | tf_op jit(solution)/shard_map/all_to_all | solution.py:137
  25.6 3.3 %all-to-all-start.1 = ((bf16[8,2,432]{2,1,0:T(2,128)(2,1)}), bf16[8,2,432]{2,1,0:T(2,128)(2,1)S(1)}, u32[]{:S(2)}, u32[]{:S(2)}) async-start(bf16[8,2,432]{2,1,0:T(2,128)(2,1)} %reshape.470), calls=%async_computation.1 | async-start | bytes 32768 | tf_op jit(solution)/shard_map/all_to_all | solution.py:138
  30.9 4.6 %all-to-all-done.1 = bf16[8,2,432]{2,1,0:T(2,128)(2,1)S(1)} async-done(((bf16[8,2,432]{2,1,0:T(2,128)(2,1)}), bf16[8,2,432]{2,1,0:T(2,128)(2,1)S(1)}, u32[]{:S(2)}, u32[]{:S(2)}) %all-to-all-start.1) | async-done | bytes 13856 | tf_op jit(solution)/shard_map/all_to_all | solution.py:138
  36.1 10.5 %all-reduce.1 = bf16[8,3,2,3,49]{4,0,3,2,1:T(8,128)(2,1)S(1)} all-reduce(bf16[8,3,2,3,49]{4,0,3,2,1:T(8,128)(2,1)S(1)} %copy.101), channel_id=2, replica_groups=mesh['wave'=8,'lev'=4] {'lev'}, use_global_device_ids=true, to_apply=%region_1.2.clone | all-reduce | flops 7056 | bytes 28224
  47.0 11.7 %all-reduce.2 = bf16[8,6,2,3,24]{4,0,3,2,1:T(8,128)(2,1)S(1)} all-reduce(bf16[8,6,2,3,24]{4,0,3,2,1:T(8,128)(2,1)S(1)} %convolution_convert_fusion), channel_id=3, replica_groups=mesh['wave'=8,'lev'=4] {'lev'}, use_global_device_ids=true, to_apply=%region_2.3.clone | all-reduce | flops 6912 | bytes 27648
  58.8 1.1 collective-permute-start.3
  59.9 1.9 %collective-permute-done = f32[2,1,2,3,24]{4,0,3,2,1:T(2,128)S(1)} collective-permute-done((f32[2,1,2,3,24]{4,0,3,2,1:T(2,128)S(1)}, f32[2,1,2,3,24]{4,0,3,2,1:T(2,128)S(1)}, u32[]{:S(2)}, u32[]{:S(2)}) %collective-permute-start) | collective-permute-done | bytes 1184 | tf_op jit(solution)/shard_map/ppermute | solution.py:21
  62.5 1.2 collective-permute-start.4
  63.6 1.3 collective-permute-done.1
  64.9 1.4 %slice.58 = f32[8,1280]{1,0:T(8,128)S(1)} slice(f32[8,2560]{1,0:T(8,128)S(1)} %copy-done.3), slice={[0:8:1], [0:2560:2]} | slice | bytes 81920 | tf_op jit(solution)/shard_map/slice | solution.py:100
  67.0 1.1 collective-permute-start.5
  69.2 3.3 %all-to-all-start.2 = ((bf16[8,1,2,3,1,24]{0,2,3,4,1,5:T(2,128)(2,1)}), bf16[8,1,2,3,1,24]{0,2,3,4,1,5:T(2,128)(2,1)S(1)}, u32[]{:S(2)}, u32[]{:S(2)}) async-start(bf16[8,1,2,3,1,24]{0,2,3,4,1,5:T(2,128)(2,1)} %copy.103), calls=%async_computation.2 | async-start | bytes 73728 | tf_op jit(solution)/shard_map/all_to_all | solution.py:126
  73.7 5.5 %all-to-all-done.2 = bf16[8,1,2,3,1,24]{0,2,3,4,1,5:T(2,128)(2,1)S(1)} async-done(((bf16[8,1,2,3,1,24]{0,2,3,4,1,5:T(2,128)(2,1)}), bf16[8,1,2,3,1,24]{0,2,3,4,1,5:T(2,128)(2,1)S(1)}, u32[]{:S(2)}, u32[]{:S(2)}) %all-to-all-start.2) | async-done | bytes 2336 | tf_op jit(solution)/shard_map/all_to_all | solution.py:126
  79.2 3.3 %all-to-all-start.4 = ((bf16[8,1,2,3,1,24]{0,2,3,4,1,5:T(2,128)(2,1)}), bf16[8,1,2,3,1,24]{0,2,3,4,1,5:T(2,128)(2,1)S(1)}, u32[]{:S(2)}, u32[]{:S(2)}) async-start(bf16[8,1,2,3,1,24]{0,2,3,4,1,5:T(2,128)(2,1)} %copy.112), calls=%async_computation.4 | async-start | bytes 73728 | tf_op jit(solution)/shard_map/all_to_all | solution.py:126
  83.7 5.5 %all-to-all-done.4 = bf16[8,1,2,3,1,24]{0,2,3,4,1,5:T(2,128)(2,1)S(1)} async-done(((bf16[8,1,2,3,1,24]{0,2,3,4,1,5:T(2,128)(2,1)}), bf16[8,1,2,3,1,24]{0,2,3,4,1,5:T(2,128)(2,1)S(1)}, u32[]{:S(2)}, u32[]{:S(2)}) %all-to-all-start.4) | async-done | bytes 2336 | tf_op jit(solution)/shard_map/all_to_all | solution.py:126
  89.2 3.3 %all-to-all-start.3 = ((bf16[8,1,2,24,1,3]{0,2,5,4,1,3:T(2,128)(2,1)}), bf16[8,1,2,24,1,3]{0,2,5,4,1,3:T(2,128)(2,1)S(1)}, u32[]{:S(2)}, u32[]{:S(2)}) async-start(bf16[8,1,2,24,1,3]{0,2,5,4,1,3:T(2,128)(2,1)} %copy.107), calls=%async_computation.3 | async-start | bytes 73728 | tf_op jit(solution)/shard_map/all_to_all | solution.py:129
  93.7 5.5 %all-to-all-done.3 = bf16[8,1,2,24,1,3]{0,2,5,4,1,3:T(2,128)(2,1)S(1)} async-done(((bf16[8,1,2,24,1,3]{0,2,5,4,1,3:T(2,128)(2,1)}), bf16[8,1,2,24,1,3]{0,2,5,4,1,3:T(2,128)(2,1)S(1)}, u32[]{:S(2)}, u32[]{:S(2)}) %all-to-all-start.3) | async-done | bytes 2336 | tf_op jit(solution)/shard_map/all_to_all | solution.py:129
  99.2 3.3 %all-to-all-start.5 = ((bf16[8,1,2,24,1,3]{0,2,5,4,1,3:T(2,128)(2,1)}), bf16[8,1,2,24,1,3]{0,2,5,4,1,3:T(2,128)(2,1)S(1)}, u32[]{:S(2)}, u32[]{:S(2)}) async-start(bf16[8,1,2,24,1,3]{0,2,5,4,1,3:T(2,128)(2,1)} %copy.116), calls=%async_computation.5 | async-start | bytes 73728 | tf_op jit(solution)/shard_map/all_to_all | solution.py:129
  103.0 6.2 %all-to-all-done.5 = bf16[8,1,2,24,1,3]{0,2,5,4,1,3:T(2,128)(2,1)S(1)} async-done(((bf16[8,1,2,24,1,3]{0,2,5,4,1,3:T(2,128)(2,1)}), bf16[8,1,2,24,1,3]{0,2,5,4,1,3:T(2,128)(2,1)S(1)}, u32[]{:S(2)}, u32[]{:S(2)}) %all-to-all-start.5) | async-done | bytes 2336 | tf_op jit(solution)/shard_map/all_to_all | solution.py:129
  109.6 10.3 %all-reduce.6 = (bf16[8,1,2,3,24]{4,0,3,2,1:T(8,128)(2,1)S(1)}, bf16[8,1,2,3,24]{4,0,3,2,1:T(8,128)(2,1)S(1)}) all-reduce(bf16[8,1,2,3,24]{4,0,3,2,1:T(8,128)(2,1)S(1)} %fusion.17, bf16[8,1,2,3,24]{4,0,3,2,1:T(8,128)(2,1)S(1)} %fusion.15), channel_id=5, replica_groups=mesh['wave'=8,'lev'=4] {'lev'}, use_global_device_ids=true, to_apply=%region_4.6.clone | all-reduce | flops 2304 | bytes 9216
  120.2 10.4 %all-reduce.5 = bf16[8,2,2,3,24]{4,0,3,2,1:T(8,128)(2,1)S(1)} all-reduce(bf16[8,2,2,3,24]{4,0,3,2,1:T(8,128)(2,1)S(1)} %convolution_convert_fusion.2), channel_id=6, replica_groups=mesh['wave'=8,'lev'=4] {'lev'}, use_global_device_ids=true, to_apply=%region_5.7.clone | all-reduce | flops 2304 | bytes 9216
  (85 shorter events, 17.0 us)
Async XLA Ops:
  0.6 46.0 %copy-start = (f32[8,8]{1,0:T(8,128)S(1)}, f32[8,8]{1,0:T(8,128)}, u32[]{:S(2)}) copy-start(f32[8,8]{1,0:T(8,128)} %param.16) | copy-start | bytes 772
  0.6 0.8 copy-start.2
  7.7 0.7 copy-start.1
  9.6 6.4 %copy-start.4 = (s32[24]{0:T(128)S(1)}, s32[24]{0:T(128)}, u32[]{:S(2)}) copy-start(s32[24]{0:T(128)} %param.11) | copy-start | bytes 292
  9.6 13.0 %all-to-all-start = ((bf16[8,2,432]{2,1,0:T(2,128)(2,1)}), bf16[8,2,432]{2,1,0:T(2,128)(2,1)S(1)}, u32[]{:S(2)}, u32[]{:S(2)}) async-start(bf16[8,2,432]{2,1,0:T(2,128)(2,1)} %reshape.468), calls=%async_computation | async-start | bytes 32768 | tf_op jit(solution)/shard_map/all_to_all | solution.py:137
  18.4 0.7 copy-start.6
  19.2 0.7 copy-start.7
  22.8 0.9 copy-start.3
  25.6 9.9 %all-to-all-start.1 = ((bf16[8,2,432]{2,1,0:T(2,128)(2,1)}), bf16[8,2,432]{2,1,0:T(2,128)(2,1)S(1)}, u32[]{:S(2)}, u32[]{:S(2)}) async-start(bf16[8,2,432]{2,1,0:T(2,128)(2,1)} %reshape.470), calls=%async_computation.1 | async-start | bytes 32768 | tf_op jit(solution)/shard_map/all_to_all | solution.py:138
  29.0 0.7 copy-start.8
  58.8 3.1 %collective-permute-start = (f32[2,1,2,3,24]{4,0,3,2,1:T(2,128)S(1)}, f32[2,1,2,3,24]{4,0,3,2,1:T(2,128)S(1)}, u32[]{:S(2)}, u32[]{:S(2)}) collective-permute-start(f32[2,1,2,3,24]{4,0,3,2,1:T(2,128)S(1)} %get-tuple-element.14), channel_id=1, source_target_pairs={{0,1},{1,2},{2,3},{3,0},{4,5},{5,6},{6,7},{7,4},{8,9},{9,10},{10,1... | collective-permute-start | bytes 3464 | tf_op jit(solution)/shard_map/ppermute | solution.py:21
  58.8 3.6 %collective-permute-start.3 = (f32[2,1,2,3,24]{4,0,3,2,1:T(2,128)S(1)}, f32[2,1,2,3,24]{4,0,3,2,1:T(2,128)S(1)}, u32[]{:S(2)}, u32[]{:S(2)}) collective-permute-start(f32[2,1,2,3,24]{4,0,3,2,1:T(2,128)S(1)} %get-tuple-element.19), channel_id=1, source_target_pairs={{0,1},{1,2},{2,3},{3,0},{4,5},{5,6},{6,7},{7,4},{8,9},{9,10},{10,1... | collective-permute-start | bytes 3464 | tf_op jit(solution)/shard_map/ppermute | solution.py:21
  61.9 3.1 %collective-permute-start.1 = (f32[2,1,2,3,24]{4,0,3,2,1:T(2,128)S(1)}, f32[2,1,2,3,24]{4,0,3,2,1:T(2,128)S(1)}, u32[]{:S(2)}, u32[]{:S(2)}) collective-permute-start(f32[2,1,2,3,24]{4,0,3,2,1:T(2,128)S(1)} %collective-permute-done), channel_id=1, source_target_pairs={{0,1},{1,2},{2,3},{3,0},{4,5},{5,6},{6,7},{7,4},{8,9},{9,10},{10,1... | collective-permute-start | bytes 3464 | tf_op jit(solution)/shard_map/ppermute | solution.py:21
  62.5 4.5 %collective-permute-start.4 = (f32[2,1,2,3,24]{4,0,3,2,1:T(2,128)S(1)}, f32[2,1,2,3,24]{4,0,3,2,1:T(2,128)S(1)}, u32[]{:S(2)}, u32[]{:S(2)}) collective-permute-start(f32[2,1,2,3,24]{4,0,3,2,1:T(2,128)S(1)} %collective-permute-done.3), channel_id=1, source_target_pairs={{0,1},{1,2},{2,3},{3,0},{4,5},{5,6},{6,7},{7,4},{8,9},{9,10},{10,1... | collective-permute-start | bytes 3464 | tf_op jit(solution)/shard_map/ppermute | solution.py:21
  64.9 3.2 %collective-permute-start.2 = (f32[2,1,2,3,24]{4,0,3,2,1:T(2,128)S(1)}, f32[2,1,2,3,24]{4,0,3,2,1:T(2,128)S(1)}, u32[]{:S(2)}, u32[]{:S(2)}) collective-permute-start(f32[2,1,2,3,24]{4,0,3,2,1:T(2,128)S(1)} %collective-permute-done.1), channel_id=1, source_target_pairs={{0,1},{1,2},{2,3},{3,0},{4,5},{5,6},{6,7},{7,4},{8,9},{9,10},{10,1... | collective-permute-start | bytes 3464 | tf_op jit(solution)/shard_map/ppermute | solution.py:21
  66.4 1.8 %copy-start.5 = (f32[8,8]{1,0:T(8,128)S(1)}, f32[8,8]{1,0:T(8,128)}, u32[]{:S(2)}) copy-start(f32[8,8]{1,0:T(8,128)} %param.15) | copy-start | bytes 772
  67.0 5.6 %collective-permute-start.5 = (f32[2,1,2,3,24]{4,0,3,2,1:T(2,128)S(1)}, f32[2,1,2,3,24]{4,0,3,2,1:T(2,128)S(1)}, u32[]{:S(2)}, u32[]{:S(2)}) collective-permute-start(f32[2,1,2,3,24]{4,0,3,2,1:T(2,128)S(1)} %collective-permute-done.4), channel_id=1, source_target_pairs={{0,1},{1,2},{2,3},{3,0},{4,5},{5,6},{6,7},{7,4},{8,9},{9,10},{10,1... | collective-permute-start | bytes 3464 | tf_op jit(solution)/shard_map/ppermute | solution.py:21
  69.2 10.0 %all-to-all-start.2 = ((bf16[8,1,2,3,1,24]{0,2,3,4,1,5:T(2,128)(2,1)}), bf16[8,1,2,3,1,24]{0,2,3,4,1,5:T(2,128)(2,1)S(1)}, u32[]{:S(2)}, u32[]{:S(2)}) async-start(bf16[8,1,2,3,1,24]{0,2,3,4,1,5:T(2,128)(2,1)} %copy.103), calls=%async_computation.2 | async-start | bytes 73728 | tf_op jit(solution)/shard_map/all_to_all | solution.py:126
  79.2 10.0 %all-to-all-start.4 = ((bf16[8,1,2,3,1,24]{0,2,3,4,1,5:T(2,128)(2,1)}), bf16[8,1,2,3,1,24]{0,2,3,4,1,5:T(2,128)(2,1)S(1)}, u32[]{:S(2)}, u32[]{:S(2)}) async-start(bf16[8,1,2,3,1,24]{0,2,3,4,1,5:T(2,128)(2,1)} %copy.112), calls=%async_computation.4 | async-start | bytes 73728 | tf_op jit(solution)/shard_map/all_to_all | solution.py:126
  89.2 10.0 %all-to-all-start.3 = ((bf16[8,1,2,24,1,3]{0,2,5,4,1,3:T(2,128)(2,1)}), bf16[8,1,2,24,1,3]{0,2,5,4,1,3:T(2,128)(2,1)S(1)}, u32[]{:S(2)}, u32[]{:S(2)}) async-start(bf16[8,1,2,24,1,3]{0,2,5,4,1,3:T(2,128)(2,1)} %copy.107), calls=%async_computation.3 | async-start | bytes 73728 | tf_op jit(solution)/shard_map/all_to_all | solution.py:129
  99.2 10.0 %all-to-all-start.5 = ((bf16[8,1,2,24,1,3]{0,2,5,4,1,3:T(2,128)(2,1)}), bf16[8,1,2,24,1,3]{0,2,5,4,1,3:T(2,128)(2,1)S(1)}, u32[]{:S(2)}, u32[]{:S(2)}) async-start(bf16[8,1,2,24,1,3]{0,2,5,4,1,3:T(2,128)(2,1)} %copy.116), calls=%async_computation.5 | async-start | bytes 73728 | tf_op jit(solution)/shard_map/all_to_all | solution.py:129
